TPU v7x, 32 devices: a whole 2x2x4 slice. The times are simulated.
32 devices in a mesh: grp: 4 (over y, x), dom: 8 (over z, core).
Axes of the slice: x: 2, y: 2, z: 4, core: 2. Of those that a mesh axis runs over, the one named last changes fastest.
Arguments:
- displacement: float32 [4, 3, 16, 96, 128], P('grp', None, 'dom'), may hold values from -3 to 3
- velocity: float32 [4, 3, 16, 96, 128], P('grp', None, 'dom'), may hold values from -6 to 6
- external: float32 [4, 3, 16, 96, 128], P('grp', None, 'dom'), may hold values from -6 to 6
- mass: float32 [4, 16, 96, 128], P('grp', 'dom'), may hold values from 1 to 3
- elem_scale: float32 [4, 16, 96, 128], P('grp', 'dom'), may hold values from 0.05 to 0.5
- stiffness: float32 [4, 24, 24], P('grp'), as said below
- substeps: int32 [4], P('grp'), may hold values from 1 to 8
- own_nodes: int32 [4, 128], P('grp', 'dom'), may hold values from 0 to 24575, as said below
- peer_nodes: int32 [4, 128], P('grp', 'dom'), may hold values from 0 to 24575, as said below
- normals: float32 [4, 3, 128], P('grp', None, 'dom'), may hold values from -4 to 4
- schur_inverse: float32 [512, 512], P(('grp', 'dom')), as said below
Outputs:
- new_displacement: float32 [4, 3, 16, 96, 128], P('grp', None, 'dom')
- new_velocity: float32 [4, 3, 16, 96, 128], P('grp', None, 'dom')
Inputs may be any that keep to these rules, and one draw needn't show every extreme that they name: `own_nodes`: the 16 entries of one device's block are distinct. `peer_nodes`: the 16 entries of one device's block are distinct. `schur_inverse`: symmetric. `stiffness`: symmetric positive definite.
All inputs are finite; a program needn't handle non-finite values.
Results may differ from a plain program's by a relative error of at most 0.0001.
Values sent between devices are 32-bit elements; how exact they have to be, the bound alone decides.
A program may use at most 64 MiB of HBM per device.

v0:
```python
import jax
import jax.numpy as jnp
from jax import lax
from jax.sharding import PartitionSpec as P

MAXSUB = 8


coarse_step = 0.4


def shifted(x, axis, by):
    length = lax.axis_size(axis)
    pairs = [(i, i + by) for i in range(length) if 0 <= i + by < length]
    return lax.ppermute(x, axis, pairs)


def shifted_2(block, axis, distance):
    devices = range(lax.axis_size(axis))
    route = [((i - distance) % len(devices), i) for i in devices]
    return lax.ppermute(block, axis, route)


def corner_stack(padded, planes):
    pieces = []
    for plane_off in (0, 1):
        for row_off in (0, 1):
            for col_off in (0, 1):
                block = padded[:, plane_off : plane_off + planes]
                block = jnp.roll(block, -row_off, axis=2)
                pieces.append(jnp.roll(block, -col_off, axis=3))
    return jnp.stack(pieces, 0).reshape(24, -1)


def element_forces(padded, scale, kmat):
    stacked = corner_stack(padded, scale.shape[0])
    forces = jnp.dot(
        kmat, stacked, precision=lax.Precision.HIGHEST, preferred_element_type=jnp.float32
    )
    forces = forces * scale.reshape(1, -1)
    return forces.reshape((8, 3) + scale.shape)


def assemble(forces):
    planes = forces.shape[2]
    total = jnp.zeros((3, planes + 1) + forces.shape[3:], jnp.float32)
    corner = 0
    for plane_off in (0, 1):
        for row_off in (0, 1):
            for col_off in (0, 1):
                part = jnp.roll(jnp.roll(forces[corner], row_off, axis=2), col_off, axis=3)
                total = total + jnp.pad(part, ((0, 0), (plane_off, 1 - plane_off), (0, 0), (0, 0)))
                corner = corner + 1
    return total


def on_device(
    displacement,
    velocity,
    external,
    mass,
    elem_scale,
    stiffness,
    substeps,
    own_nodes,
    peer_nodes,
    normals,
    schur_inverse,
):
    field = displacement[0]
    speed = velocity[0]
    loads = external[0]
    weight = mass[0]
    scale = elem_scale[0]
    kmat = stiffness[0]
    count = substeps[0]
    delta = coarse_step / count.astype(jnp.float32)

    def internal(state_field):
        upper = shifted(state_field[:, :1], "dom", -1)
        padded = jnp.concatenate([state_field, upper], 1)
        nodal = assemble(element_forces(padded, scale, kmat))
        carried = shifted(nodal[:, -1:], "dom", 1)
        return nodal[:, :-1] + jnp.pad(carried, ((0, 0), (0, nodal.shape[1] - 2), (0, 0), (0, 0)))

    def advance(step, state):
        state_field, state_speed = state
        accel = (loads - internal(state_field)) / weight
        next_speed = state_speed + delta * accel
        next_field = state_field + delta * next_speed
        active = step < count
        return (
            jnp.where(active, next_field, state_field),
            jnp.where(active, next_speed, state_speed),
        )

    field, speed = lax.fori_loop(0, MAXSUB, advance, (field, speed))
    flat_speed = speed.reshape(3, -1)
    masses = weight.reshape(-1)
    own = own_nodes[0]
    peer = peer_nodes[0]
    direction = normals[0]
    own_speed = flat_speed[:, own]
    far_speed = shifted_2(flat_speed[:, peer], "grp", -1)
    gap = jnp.sum(direction * (own_speed - far_speed), axis=0)
    multiplier = jnp.dot(
        schur_inverse,
        lax.all_gather(gap, ("grp", "dom"), axis=0, tiled=True),
        precision=lax.Precision.HIGHEST,
        preferred_element_type=jnp.float32,
    )
    correction = multiplier[None, :] * direction
    incoming = shifted_2(correction, "grp", 1)
    flat_speed = flat_speed.at[:, own].add(-correction / masses[own][None, :])
    flat_speed = flat_speed.at[:, peer].add(incoming / masses[peer][None, :])
    return (field[None], flat_speed.reshape(speed.shape)[None])


def solution(mesh):
    return jax.shard_map(
        on_device,
        mesh=mesh,
        in_specs=(
            P("grp", None, "dom", None, None),
            P("grp", None, "dom", None, None),
            P("grp", None, "dom", None, None),
            P("grp", "dom", None, None),
            P("grp", "dom", None, None),
            P("grp", None, None),
            P("grp"),
            P("grp", "dom"),
            P("grp", "dom"),
            P("grp", None, "dom"),
            P(("grp", "dom"), None),
        ),
        out_specs=(P("grp", None, "dom", None, None), P("grp", None, "dom", None, None)),
        check_vma=False,
    )
```

profile of v0, /device:TPU:0, one launch (start us, length us, event | category | flops | bytes accessed | tf_op | source)
XLA Modules:
  0.0 270.4 jit_solution(12340849130333921923)
XLA Ops:
  0.6 1.0 copy.78
  1.6 1.0 copy.79
  3.9 172.7 %while.17 = (s32[]{:T(128)}, f32[3,2,96,128]{3,2,1,0:T(8,128)S(1)}, f32[3,2,96,128]{3,2,1,0:T(8,128)S(1)}, s32[]{:T(128)}, f32[]{:T(128)}, /*index=5*/f32[24,24]...) while((s32[]{:T(128)}, f32[3,2,96,128]{3,2,1,0:T(8,128)S(1)}, ...), condition=%wide.region_1.2_spmd, body=%wide.region_0.1_spmd.sunk | while | flops 175142016 | bytes 37897272 | solution.py:97
  4.0 1.3 collective-permute-start
  8.0 0.9 fusion.54
  12.5 1.9 reshape.150
  14.4 2.2 fusion.61
  18.4 4.9 %collective-permute-start.1 = (f32[3,1,96,128]{3,2,1,0:T(8,128)S(1)}, f32[3,1,96,128]{3,2,1,0:T(8,128)S(1)}, u32[]{:S(2)}, u32[]{:S(2)}) collective-permute-start(f32[3,1,96,128]{3,2,1,0:T(8,128)S(1)} %slice.573), channel_id=1, source_target_pairs={{0,1},{1,2},{2,3},{3,4},{4,5},{5,6},{6,7},{8,9},{9,10},{10,11},{11... | collective-permute-start | bytes 442376 | tf_op jit(solution)/shard_map/while/body/eval_jaxpr/ppermute | solution.py:15
  24.5 1.3 collective-permute-start
  28.5 0.9 fusion.54
  33.0 1.9 reshape.150
  35.0 2.2 fusion.61
  39.0 6.1 %collective-permute-start.1 = (f32[3,1,96,128]{3,2,1,0:T(8,128)S(1)}, f32[3,1,96,128]{3,2,1,0:T(8,128)S(1)}, u32[]{:S(2)}, u32[]{:S(2)}) collective-permute-start(f32[3,1,96,128]{3,2,1,0:T(8,128)S(1)} %slice.573), channel_id=1, source_target_pairs={{0,1},{1,2},{2,3},{3,4},{4,5},{5,6},{6,7},{8,9},{9,10},{10,11},{11... | collective-permute-start | bytes 442376 | tf_op jit(solution)/shard_map/while/body/eval_jaxpr/ppermute | solution.py:15
  46.3 1.3 collective-permute-start
  50.3 0.9 fusion.54
  54.8 1.9 reshape.150
  56.7 2.2 fusion.61
  60.7 6.1 %collective-permute-start.1 = (f32[3,1,96,128]{3,2,1,0:T(8,128)S(1)}, f32[3,1,96,128]{3,2,1,0:T(8,128)S(1)}, u32[]{:S(2)}, u32[]{:S(2)}) collective-permute-start(f32[3,1,96,128]{3,2,1,0:T(8,128)S(1)} %slice.573), channel_id=1, source_target_pairs={{0,1},{1,2},{2,3},{3,4},{4,5},{5,6},{6,7},{8,9},{9,10},{10,11},{11... | collective-permute-start | bytes 442376 | tf_op jit(solution)/shard_map/while/body/eval_jaxpr/ppermute | solution.py:15
  68.0 1.3 collective-permute-start
  72.0 0.9 fusion.54
  76.5 1.9 reshape.150
  78.5 2.2 fusion.61
  82.5 6.1 %collective-permute-start.1 = (f32[3,1,96,128]{3,2,1,0:T(8,128)S(1)}, f32[3,1,96,128]{3,2,1,0:T(8,128)S(1)}, u32[]{:S(2)}, u32[]{:S(2)}) collective-permute-start(f32[3,1,96,128]{3,2,1,0:T(8,128)S(1)} %slice.573), channel_id=1, source_target_pairs={{0,1},{1,2},{2,3},{3,4},{4,5},{5,6},{6,7},{8,9},{9,10},{10,11},{11... | collective-permute-start | bytes 442376 | tf_op jit(solution)/shard_map/while/body/eval_jaxpr/ppermute | solution.py:15
  89.8 1.3 collective-permute-start
  98.3 1.9 reshape.150
  100.2 2.2 fusion.61
  104.2 6.1 %collective-permute-start.1 = (f32[3,1,96,128]{3,2,1,0:T(8,128)S(1)}, f32[3,1,96,128]{3,2,1,0:T(8,128)S(1)}, u32[]{:S(2)}, u32[]{:S(2)}) collective-permute-start(f32[3,1,96,128]{3,2,1,0:T(8,128)S(1)} %slice.573), channel_id=1, source_target_pairs={{0,1},{1,2},{2,3},{3,4},{4,5},{5,6},{6,7},{8,9},{9,10},{10,11},{11... | collective-permute-start | bytes 442376 | tf_op jit(solution)/shard_map/while/body/eval_jaxpr/ppermute | solution.py:15
  111.5 1.3 collective-permute-start
  120.0 1.9 reshape.150
  121.9 2.2 fusion.61
  125.9 6.1 %collective-permute-start.1 = (f32[3,1,96,128]{3,2,1,0:T(8,128)S(1)}, f32[3,1,96,128]{3,2,1,0:T(8,128)S(1)}, u32[]{:S(2)}, u32[]{:S(2)}) collective-permute-start(f32[3,1,96,128]{3,2,1,0:T(8,128)S(1)} %slice.573), channel_id=1, source_target_pairs={{0,1},{1,2},{2,3},{3,4},{4,5},{5,6},{6,7},{8,9},{9,10},{10,11},{11... | collective-permute-start | bytes 442376 | tf_op jit(solution)/shard_map/while/body/eval_jaxpr/ppermute | solution.py:15
  133.2 1.3 collective-permute-start
  141.7 1.9 reshape.150
  143.7 2.2 fusion.61
  147.7 6.1 %collective-permute-start.1 = (f32[3,1,96,128]{3,2,1,0:T(8,128)S(1)}, f32[3,1,96,128]{3,2,1,0:T(8,128)S(1)}, u32[]{:S(2)}, u32[]{:S(2)}) collective-permute-start(f32[3,1,96,128]{3,2,1,0:T(8,128)S(1)} %slice.573), channel_id=1, source_target_pairs={{0,1},{1,2},{2,3},{3,4},{4,5},{5,6},{6,7},{8,9},{9,10},{10,11},{11... | collective-permute-start | bytes 442376 | tf_op jit(solution)/shard_map/while/body/eval_jaxpr/ppermute | solution.py:15
  155.0 1.3 collective-permute-start
  163.5 1.9 reshape.150
  165.4 2.2 fusion.61
  169.4 6.1 %collective-permute-start.1 = (f32[3,1,96,128]{3,2,1,0:T(8,128)S(1)}, f32[3,1,96,128]{3,2,1,0:T(8,128)S(1)}, u32[]{:S(2)}, u32[]{:S(2)}) collective-permute-start(f32[3,1,96,128]{3,2,1,0:T(8,128)S(1)} %slice.573), channel_id=1, source_target_pairs={{0,1},{1,2},{2,3},{3,4},{4,5},{5,6},{6,7},{8,9},{9,10},{10,11},{11... | collective-permute-start | bytes 442376 | tf_op jit(solution)/shard_map/while/body/eval_jaxpr/ppermute | solution.py:15
  176.7 6.6 %copy.18 = f32[3,2,96,128]{0,3,2,1:T(8,128)} copy(f32[3,2,96,128]{3,2,1,0:T(8,128)S(1)} %get-tuple-element.224) | data formatting | bytes 589824 | tf_op jit(solution)/shard_map/while | solution.py:97
  183.4 5.1 %gather_fusion.1 = f32[16,3]{1,0:T(8,128)S(1)} fusion(f32[3,24576]{0,1:T(8,128)} %bitcast.189, s32[1024]{0:T(1024)S(1)} %pad_clamp_fusion), kind=kCustom, calls=%fused_computation.1 | custom fusion | bytes 448 | tf_op jit(solution)/shard_map/gather | solution.py:104
  188.5 2.5 collective-permute-start.2
  192.3 5.1 %gather_fusion = f32[16,3]{1,0:T(8,128)S(1)} fusion(f32[3,24576]{0,1:T(8,128)} %bitcast.190, s32[1024]{0:T(1024)S(1)} %pad_clamp_fusion.1), kind=kCustom, calls=%fused_computation | custom fusion | bytes 448 | tf_op jit(solution)/shard_map/gather | solution.py:103
  198.0 42.1 %all-reduce.9 = f32[512]{0:T(512)S(1)} all-reduce(f32[512]{0:T(512)S(1)} %dynamic-update-slice), channel_id=1, replica_groups=mesh['grp'=4,'dom'=8] {'grp','dom'}, use_global_device_ids=true, to_apply=%add.9 | all-reduce | flops 512 | bytes 4096
  240.2 2.3 collective-permute-start.3
  242.7 9.7 %scatter_fusion = f32[3,24576]{0,1:T(8,128)} fusion(f32[3,24576]{0,1:T(8,128)} %bitcast.191, s32[16]{0:T(128)S(1)} %fusion.27, f32[16,3]{1,0:T(8,128)S(1)} %copy.20), kind=kCustom, calls=%fused_computation.4 | custom fusion | flops 48 | bytes 640 | tf_op jit(solution)/shard_map/scatter-add | solution.py:114
  252.5 9.7 %scatter_fusion.1 = f32[3,24576]{0,1:T(8,128)} fusion(f32[3,24576]{0,1:T(8,128)} %scatter_fusion, s32[16]{0:T(128)S(1)} %fusion.28, f32[16,3]{1,0:T(8,128)S(1)} %copy.21), kind=kCustom, calls=%fused_computation.5 | custom fusion | flops 48 | bytes 640 | tf_op jit(solution)/shard_map/scatter-add | solution.py:115
  262.2 8.3 %copy.22 = f32[1,3,2,96,128]{4,3,2,1,0:T(8,128)} copy(f32[1,3,2,96,128]{1,4,3,2,0:T(8,128)} %bitcast.192) | data formatting | bytes 589824
  (432 shorter events, 73.4 us)
Async XLA Ops:
  0.6 239.5 %copy-start = (f32[16,512]{1,0:T(8,128)S(1)}, f32[16,512]{1,0:T(8,128)}, u32[]{:S(2)}) copy-start(f32[16,512]{1,0:T(8,128)} %param.23) | copy-start | bytes 98308
  4.0 4.9 %collective-permute-start = (f32[3,1,96,128]{3,2,1,0:T(8,128)S(1)}, f32[3,1,96,128]{3,2,1,0:T(8,128)S(1)}, u32[]{:S(2)}, u32[]{:S(2)}) collective-permute-start(f32[3,1,96,128]{3,2,1,0:T(8,128)S(1)} %slice.562), channel_id=1, source_target_pairs={{1,0},{2,1},{3,2},{4,3},{5,4},{6,5},{7,6},{9,8},{10,9},{11,10},{12... | collective-permute-start | bytes 442376 | tf_op jit(solution)/shard_map/while/body/eval_jaxpr/ppermute | solution.py:15
  12.5 1.9 copy-start.5
  12.5 1.9 copy-start.6
  18.0 6.4 %copy-start.2 = (f32[1,2,96,128]{3,2,1,0:T(8,128)S(1)}, f32[1,2,96,128]{3,2,1,0:T(8,128)}, u32[]{:S(2)}) copy-start(f32[1,2,96,128]{3,2,1,0:T(8,128)} %get-tuple-element.368) | copy-start | bytes 294916 | tf_op jit(solution)/shard_map/while
  18.0 6.3 %copy-start.4 = (f32[3,2,96,128]{3,2,1,0:T(8,128)S(1)}, f32[3,2,96,128]{3,2,1,0:T(8,128)}, u32[]{:S(2)}) copy-start(f32[3,2,96,128]{3,2,1,0:T(8,128)} %get-tuple-element.367) | copy-start | bytes 884740 | tf_op jit(solution)/shard_map/while
  18.4 5.9 %collective-permute-start.1 = (f32[3,1,96,128]{3,2,1,0:T(8,128)S(1)}, f32[3,1,96,128]{3,2,1,0:T(8,128)S(1)}, u32[]{:S(2)}, u32[]{:S(2)}) collective-permute-start(f32[3,1,96,128]{3,2,1,0:T(8,128)S(1)} %slice.573), channel_id=1, source_target_pairs={{0,1},{1,2},{2,3},{3,4},{4,5},{5,6},{6,7},{8,9},{9,10},{10,11},{11... | collective-permute-start | bytes 442376 | tf_op jit(solution)/shard_map/while/body/eval_jaxpr/ppermute | solution.py:15
  24.5 4.9 %collective-permute-start = (f32[3,1,96,128]{3,2,1,0:T(8,128)S(1)}, f32[3,1,96,128]{3,2,1,0:T(8,128)S(1)}, u32[]{:S(2)}, u32[]{:S(2)}) collective-permute-start(f32[3,1,96,128]{3,2,1,0:T(8,128)S(1)} %slice.562), channel_id=1, source_target_pairs={{1,0},{2,1},{3,2},{4,3},{5,4},{6,5},{7,6},{9,8},{10,9},{11,10},{12... | collective-permute-start | bytes 442376 | tf_op jit(solution)/shard_map/while/body/eval_jaxpr/ppermute | solution.py:15
  33.0 1.9 copy-start.6
  38.5 7.5 %copy-start.2 = (f32[1,2,96,128]{3,2,1,0:T(8,128)S(1)}, f32[1,2,96,128]{3,2,1,0:T(8,128)}, u32[]{:S(2)}) copy-start(f32[1,2,96,128]{3,2,1,0:T(8,128)} %get-tuple-element.368) | copy-start | bytes 294916 | tf_op jit(solution)/shard_map/while
  38.5 7.5 %copy-start.4 = (f32[3,2,96,128]{3,2,1,0:T(8,128)S(1)}, f32[3,2,96,128]{3,2,1,0:T(8,128)}, u32[]{:S(2)}) copy-start(f32[3,2,96,128]{3,2,1,0:T(8,128)} %get-tuple-element.367) | copy-start | bytes 884740 | tf_op jit(solution)/shard_map/while
  39.0 7.1 %collective-permute-start.1 = (f32[3,1,96,128]{3,2,1,0:T(8,128)S(1)}, f32[3,1,96,128]{3,2,1,0:T(8,128)S(1)}, u32[]{:S(2)}, u32[]{:S(2)}) collective-permute-start(f32[3,1,96,128]{3,2,1,0:T(8,128)S(1)} %slice.573), channel_id=1, source_target_pairs={{0,1},{1,2},{2,3},{3,4},{4,5},{5,6},{6,7},{8,9},{9,10},{10,11},{11... | collective-permute-start | bytes 442376 | tf_op jit(solution)/shard_map/while/body/eval_jaxpr/ppermute | solution.py:15
  46.3 4.9 %collective-permute-start = (f32[3,1,96,128]{3,2,1,0:T(8,128)S(1)}, f32[3,1,96,128]{3,2,1,0:T(8,128)S(1)}, u32[]{:S(2)}, u32[]{:S(2)}) collective-permute-start(f32[3,1,96,128]{3,2,1,0:T(8,128)S(1)} %slice.562), channel_id=1, source_target_pairs={{1,0},{2,1},{3,2},{4,3},{5,4},{6,5},{7,6},{9,8},{10,9},{11,10},{12... | collective-permute-start | bytes 442376 | tf_op jit(solution)/shard_map/while/body/eval_jaxpr/ppermute | solution.py:15
  54.8 1.9 copy-start.6
  60.3 7.5 %copy-start.2 = (f32[1,2,96,128]{3,2,1,0:T(8,128)S(1)}, f32[1,2,96,128]{3,2,1,0:T(8,128)}, u32[]{:S(2)}) copy-start(f32[1,2,96,128]{3,2,1,0:T(8,128)} %get-tuple-element.368) | copy-start | bytes 294916 | tf_op jit(solution)/shard_map/while
  60.3 7.5 %copy-start.4 = (f32[3,2,96,128]{3,2,1,0:T(8,128)S(1)}, f32[3,2,96,128]{3,2,1,0:T(8,128)}, u32[]{:S(2)}) copy-start(f32[3,2,96,128]{3,2,1,0:T(8,128)} %get-tuple-element.367) | copy-start | bytes 884740 | tf_op jit(solution)/shard_map/while
  60.7 7.1 %collective-permute-start.1 = (f32[3,1,96,128]{3,2,1,0:T(8,128)S(1)}, f32[3,1,96,128]{3,2,1,0:T(8,128)S(1)}, u32[]{:S(2)}, u32[]{:S(2)}) collective-permute-start(f32[3,1,96,128]{3,2,1,0:T(8,128)S(1)} %slice.573), channel_id=1, source_target_pairs={{0,1},{1,2},{2,3},{3,4},{4,5},{5,6},{6,7},{8,9},{9,10},{10,11},{11... | collective-permute-start | bytes 442376 | tf_op jit(solution)/shard_map/while/body/eval_jaxpr/ppermute | solution.py:15
  68.0 4.9 %collective-permute-start = (f32[3,1,96,128]{3,2,1,0:T(8,128)S(1)}, f32[3,1,96,128]{3,2,1,0:T(8,128)S(1)}, u32[]{:S(2)}, u32[]{:S(2)}) collective-permute-start(f32[3,1,96,128]{3,2,1,0:T(8,128)S(1)} %slice.562), channel_id=1, source_target_pairs={{1,0},{2,1},{3,2},{4,3},{5,4},{6,5},{7,6},{9,8},{10,9},{11,10},{12... | collective-permute-start | bytes 442376 | tf_op jit(solution)/shard_map/while/body/eval_jaxpr/ppermute | solution.py:15
  76.5 1.9 copy-start.6
  82.0 7.5 %copy-start.2 = (f32[1,2,96,128]{3,2,1,0:T(8,128)S(1)}, f32[1,2,96,128]{3,2,1,0:T(8,128)}, u32[]{:S(2)}) copy-start(f32[1,2,96,128]{3,2,1,0:T(8,128)} %get-tuple-element.368) | copy-start | bytes 294916 | tf_op jit(solution)/shard_map/while
  82.0 7.5 %copy-start.4 = (f32[3,2,96,128]{3,2,1,0:T(8,128)S(1)}, f32[3,2,96,128]{3,2,1,0:T(8,128)}, u32[]{:S(2)}) copy-start(f32[3,2,96,128]{3,2,1,0:T(8,128)} %get-tuple-element.367) | copy-start | bytes 884740 | tf_op jit(solution)/shard_map/while
  82.5 7.1 %collective-permute-start.1 = (f32[3,1,96,128]{3,2,1,0:T(8,128)S(1)}, f32[3,1,96,128]{3,2,1,0:T(8,128)S(1)}, u32[]{:S(2)}, u32[]{:S(2)}) collective-permute-start(f32[3,1,96,128]{3,2,1,0:T(8,128)S(1)} %slice.573), channel_id=1, source_target_pairs={{0,1},{1,2},{2,3},{3,4},{4,5},{5,6},{6,7},{8,9},{9,10},{10,11},{11... | collective-permute-start | bytes 442376 | tf_op jit(solution)/shard_map/while/body/eval_jaxpr/ppermute | solution.py:15
  89.8 4.9 %collective-permute-start = (f32[3,1,96,128]{3,2,1,0:T(8,128)S(1)}, f32[3,1,96,128]{3,2,1,0:T(8,128)S(1)}, u32[]{:S(2)}, u32[]{:S(2)}) collective-permute-start(f32[3,1,96,128]{3,2,1,0:T(8,128)S(1)} %slice.562), channel_id=1, source_target_pairs={{1,0},{2,1},{3,2},{4,3},{5,4},{6,5},{7,6},{9,8},{10,9},{11,10},{12... | collective-permute-start | bytes 442376 | tf_op jit(solution)/shard_map/while/body/eval_jaxpr/ppermute | solution.py:15
  98.3 1.9 copy-start.6
  103.8 7.5 %copy-start.2 = (f32[1,2,96,128]{3,2,1,0:T(8,128)S(1)}, f32[1,2,96,128]{3,2,1,0:T(8,128)}, u32[]{:S(2)}) copy-start(f32[1,2,96,128]{3,2,1,0:T(8,128)} %get-tuple-element.368) | copy-start | bytes 294916 | tf_op jit(solution)/shard_map/while
  103.8 7.5 %copy-start.4 = (f32[3,2,96,128]{3,2,1,0:T(8,128)S(1)}, f32[3,2,96,128]{3,2,1,0:T(8,128)}, u32[]{:S(2)}) copy-start(f32[3,2,96,128]{3,2,1,0:T(8,128)} %get-tuple-element.367) | copy-start | bytes 884740 | tf_op jit(solution)/shard_map/while
  104.2 7.1 %collective-permute-start.1 = (f32[3,1,96,128]{3,2,1,0:T(8,128)S(1)}, f32[3,1,96,128]{3,2,1,0:T(8,128)S(1)}, u32[]{:S(2)}, u32[]{:S(2)}) collective-permute-start(f32[3,1,96,128]{3,2,1,0:T(8,128)S(1)} %slice.573), channel_id=1, source_target_pairs={{0,1},{1,2},{2,3},{3,4},{4,5},{5,6},{6,7},{8,9},{9,10},{10,11},{11... | collective-permute-start | bytes 442376 | tf_op jit(solution)/shard_map/while/body/eval_jaxpr/ppermute | solution.py:15
  111.5 4.9 %collective-permute-start = (f32[3,1,96,128]{3,2,1,0:T(8,128)S(1)}, f32[3,1,96,128]{3,2,1,0:T(8,128)S(1)}, u32[]{:S(2)}, u32[]{:S(2)}) collective-permute-start(f32[3,1,96,128]{3,2,1,0:T(8,128)S(1)} %slice.562), channel_id=1, source_target_pairs={{1,0},{2,1},{3,2},{4,3},{5,4},{6,5},{7,6},{9,8},{10,9},{11,10},{12... | collective-permute-start | bytes 442376 | tf_op jit(solution)/shard_map/while/body/eval_jaxpr/ppermute | solution.py:15
  120.0 1.9 copy-start.6
  125.5 7.5 %copy-start.2 = (f32[1,2,96,128]{3,2,1,0:T(8,128)S(1)}, f32[1,2,96,128]{3,2,1,0:T(8,128)}, u32[]{:S(2)}) copy-start(f32[1,2,96,128]{3,2,1,0:T(8,128)} %get-tuple-element.368) | copy-start | bytes 294916 | tf_op jit(solution)/shard_map/while
  125.5 7.5 %copy-start.4 = (f32[3,2,96,128]{3,2,1,0:T(8,128)S(1)}, f32[3,2,96,128]{3,2,1,0:T(8,128)}, u32[]{:S(2)}) copy-start(f32[3,2,96,128]{3,2,1,0:T(8,128)} %get-tuple-element.367) | copy-start | bytes 884740 | tf_op jit(solution)/shard_map/while
  125.9 7.1 %collective-permute-start.1 = (f32[3,1,96,128]{3,2,1,0:T(8,128)S(1)}, f32[3,1,96,128]{3,2,1,0:T(8,128)S(1)}, u32[]{:S(2)}, u32[]{:S(2)}) collective-permute-start(f32[3,1,96,128]{3,2,1,0:T(8,128)S(1)} %slice.573), channel_id=1, source_target_pairs={{0,1},{1,2},{2,3},{3,4},{4,5},{5,6},{6,7},{8,9},{9,10},{10,11},{11... | collective-permute-start | bytes 442376 | tf_op jit(solution)/shard_map/while/body/eval_jaxpr/ppermute | solution.py:15
  133.2 4.9 %collective-permute-start = (f32[3,1,96,128]{3,2,1,0:T(8,128)S(1)}, f32[3,1,96,128]{3,2,1,0:T(8,128)S(1)}, u32[]{:S(2)}, u32[]{:S(2)}) collective-permute-start(f32[3,1,96,128]{3,2,1,0:T(8,128)S(1)} %slice.562), channel_id=1, source_target_pairs={{1,0},{2,1},{3,2},{4,3},{5,4},{6,5},{7,6},{9,8},{10,9},{11,10},{12... | collective-permute-start | bytes 442376 | tf_op jit(solution)/shard_map/while/body/eval_jaxpr/ppermute | solution.py:15
  141.7 1.9 copy-start.6
  147.2 7.5 %copy-start.2 = (f32[1,2,96,128]{3,2,1,0:T(8,128)S(1)}, f32[1,2,96,128]{3,2,1,0:T(8,128)}, u32[]{:S(2)}) copy-start(f32[1,2,96,128]{3,2,1,0:T(8,128)} %get-tuple-element.368) | copy-start | bytes 294916 | tf_op jit(solution)/shard_map/while
  147.2 7.5 %copy-start.4 = (f32[3,2,96,128]{3,2,1,0:T(8,128)S(1)}, f32[3,2,96,128]{3,2,1,0:T(8,128)}, u32[]{:S(2)}) copy-start(f32[3,2,96,128]{3,2,1,0:T(8,128)} %get-tuple-element.367) | copy-start | bytes 884740 | tf_op jit(solution)/shard_map/while
  147.7 7.1 %collective-permute-start.1 = (f32[3,1,96,128]{3,2,1,0:T(8,128)S(1)}, f32[3,1,96,128]{3,2,1,0:T(8,128)S(1)}, u32[]{:S(2)}, u32[]{:S(2)}) collective-permute-start(f32[3,1,96,128]{3,2,1,0:T(8,128)S(1)} %slice.573), channel_id=1, source_target_pairs={{0,1},{1,2},{2,3},{3,4},{4,5},{5,6},{6,7},{8,9},{9,10},{10,11},{11... | collective-permute-start | bytes 442376 | tf_op jit(solution)/shard_map/while/body/eval_jaxpr/ppermute | solution.py:15
  155.0 4.9 %collective-permute-start = (f32[3,1,96,128]{3,2,1,0:T(8,128)S(1)}, f32[3,1,96,128]{3,2,1,0:T(8,128)S(1)}, u32[]{:S(2)}, u32[]{:S(2)}) collective-permute-start(f32[3,1,96,128]{3,2,1,0:T(8,128)S(1)} %slice.562), channel_id=1, source_target_pairs={{1,0},{2,1},{3,2},{4,3},{5,4},{6,5},{7,6},{9,8},{10,9},{11,10},{12... | collective-permute-start | bytes 442376 | tf_op jit(solution)/shard_map/while/body/eval_jaxpr/ppermute | solution.py:15
  163.5 1.9 copy-start.6
  169.0 7.5 %copy-start.2 = (f32[1,2,96,128]{3,2,1,0:T(8,128)S(1)}, f32[1,2,96,128]{3,2,1,0:T(8,128)}, u32[]{:S(2)}) copy-start(f32[1,2,96,128]{3,2,1,0:T(8,128)} %get-tuple-element.368) | copy-start | bytes 294916 | tf_op jit(solution)/shard_map/while
  169.0 7.5 %copy-start.4 = (f32[3,2,96,128]{3,2,1,0:T(8,128)S(1)}, f32[3,2,96,128]{3,2,1,0:T(8,128)}, u32[]{:S(2)}) copy-start(f32[3,2,96,128]{3,2,1,0:T(8,128)} %get-tuple-element.367) | copy-start | bytes 884740 | tf_op jit(solution)/shard_map/while
  169.4 7.1 %collective-permute-start.1 = (f32[3,1,96,128]{3,2,1,0:T(8,128)S(1)}, f32[3,1,96,128]{3,2,1,0:T(8,128)S(1)}, u32[]{:S(2)}, u32[]{:S(2)}) collective-permute-start(f32[3,1,96,128]{3,2,1,0:T(8,128)S(1)} %slice.573), channel_id=1, source_target_pairs={{0,1},{1,2},{2,3},{3,4},{4,5},{5,6},{6,7},{8,9},{9,10},{10,11},{11... | collective-permute-start | bytes 442376 | tf_op jit(solution)/shard_map/while/body/eval_jaxpr/ppermute | solution.py:15
  176.7 6.7 %copy-start.1 = (f32[3,2,96,128]{3,2,1,0:T(8,128)}, f32[3,2,96,128]{3,2,1,0:T(8,128)S(1)}, u32[]{:S(2)}) copy-start(f32[3,2,96,128]{3,2,1,0:T(8,128)S(1)} %get-tuple-element.223) | copy-start | bytes 884740
  176.7 14.3 %copy-start.8 = (s32[1,16]{1,0:T(1,128)S(1)}, s32[1,16]{1,0:T(1,128)}, u32[]{:S(2)}) copy-start(s32[1,16]{1,0:T(1,128)} %param.20) | copy-start | bytes 196
  176.7 14.3 %copy-start.3 = (f32[1,2,96,128]{3,2,1,0:T(8,128)S(1)}, f32[1,2,96,128]{3,2,1,0:T(8,128)}, u32[]{:S(2)}) copy-start(f32[1,2,96,128]{3,2,1,0:T(8,128)} %get-tuple-element.370) | copy-start | bytes 294916
  176.7 20.8 %copy-start.7 = (f32[1,3,16]{2,0,1:T(1,128)S(1)}, f32[1,3,16]{2,0,1:T(1,128)}, u32[]{:S(2)}) copy-start(f32[1,3,16]{2,0,1:T(1,128)} %param.22) | copy-start | bytes 580
  188.5 9.1 %collective-permute-start.2 = (f32[3,16]{0,1:T(8,128)S(1)}, f32[3,16]{0,1:T(8,128)S(1)}, u32[]{:S(2)}, u32[]{:S(2)}) collective-permute-start(f32[3,16]{0,1:T(8,128)S(1)} %bitcast.208), channel_id=1, source_target_pairs={{8,0},{16,8},{24,16},{0,24},{9,1},{17,9},{25,17},{1,25},{10,2},{18... | collective-permute-start | bytes 584 | tf_op jit(solution)/shard_map/ppermute | solution.py:21
  240.2 12.1 %collective-permute-start.3 = (f32[3,16]{1,0:T(4,128)S(1)}, f32[3,16]{1,0:T(4,128)S(1)}, u32[]{:S(2)}, u32[]{:S(2)}) collective-permute-start(f32[3,16]{1,0:T(4,128)S(1)} %get-tuple-element.259), channel_id=1, source_target_pairs={{24,0},{0,8},{8,16},{16,24},{25,1},{1,9},{9,17},{17,25},{26,2},{2,... | collective-permute-start | bytes 584 | tf_op jit(solution)/shard_map/ppermute | solution.py:21
  (7 other events, 13.5 us)
where the time goes:
time: 272 us; the launch traced here: 270 us
  other arithmetic  68.5 us (25%)
  local copies, waits for them, and re-layouts  67.4 us (25%)
  starting transfers between devices  62.8 us (23%)
  blocking collectives  42.1 us (15%)
  matrix products  17.7 us (7%)
  loops' own time  7.78 us (3%)
    ppermute x16, starting transfers between devices, shifted(): return lax.ppermute(x, axis, pairs)  58 us
    unnamed x1, blocking collectives  42.1 us
    while x40, other arithmetic  32.4 us
    while x160, local copies, waits for them, and re-layouts  17.8 us
    dot_general x8, matrix products, element_forces(): jnp.dot(kmat, stacked, precision=lax.Precision.HIGHEST, preferred_element...  17.6 us
    reshape x8, local copies, waits for them, and re-layouts, corner_stack(): return jnp.stack(pieces, 0).reshape(24, -1)  15.3 us
    unnamed x16, local copies, waits for them, and re-layouts  10.5 us
    scatter-add x1, other arithmetic, on_device(): flat_speed = flat_speed.at[:, peer].add(incoming / masses[peer][None, :])  9.72 us
  transfers between devices with their start and end apart: 18, of which 8 were waited for; matrix products, arithmetic and copies ran while one was open for 17% of the time, Pallas kernels for 0%

commit v1 on v0

v1 whole, which is shorter than its diff:
```python
import functools

import jax
import jax.numpy as jnp
from jax import lax
from jax.experimental import pallas as pl
from jax.experimental.pallas import tpu as pltpu
from jax.sharding import PartitionSpec as P

MAXSUB = 8
MESH = pl.DeviceIdType.MESH
HIGH = lax.Precision.HIGHEST
F32 = jnp.float32
BF16 = jnp.bfloat16

coarse_step = 0.4

BLOCK = 8
WINDOW = 16
OUT_HALF = 12 * BLOCK
IN_HALF = 6 * WINDOW


def iota(shape, dim):
    return lax.broadcasted_iota(jnp.int32, shape, dim)


def halves(x):
    high = x.astype(BF16)
    return high, (x - high.astype(F32)).astype(BF16)


def block_matrix(kmat):
    outs, ins = 2 * OUT_HALF, 2 * IN_HALF

    def out_parts(q):
        a = (q >= OUT_HALF).astype(jnp.int32)
        q = q - a * OUT_HALF
        b = (q >= OUT_HALF // 2).astype(jnp.int32)
        q = q - b * (OUT_HALF // 2)
        return a, b, q >> 4, (q >> 3) & 1, q & 7

    def in_parts(q):
        a = (q >= IN_HALF).astype(jnp.int32)
        q = q - a * IN_HALF
        return a, q >> 5, (q >> 4) & 1, q & 15

    a, b, comp, e, _ = out_parts(iota((outs, 24), 0))
    pick = (iota((outs, 24), 1) == 3 * (4 * a + 2 * b + e) + comp).astype(F32)
    left = jnp.dot(pick, kmat, precision=HIGH, preferred_element_type=F32)
    row = out_parts(iota((outs, ins), 0))[4]
    window_row = in_parts(iota((outs, ins), 1))[3]
    total = jnp.zeros((outs, ins), F32)
    a, comp, e, _ = in_parts(iota((24, ins), 1))
    for b in (0, 1):
        place = (iota((24, ins), 0) == 3 * (4 * a + 2 * b + e) + comp).astype(F32)
        spread = jnp.dot(left, place, precision=HIGH, preferred_element_type=F32)
        total = jnp.where(window_row - row == b, spread, total)
    return total


def kernel(
    dims, disp, vel, ext, mass, scale, stiff, sub, own, peer, norm, schur,
    o_u, o_v,
    split_hi, split_lo, force, halo, scale_low, minv, amat, norm_own, norm_prev, schur_prev,
    parts, picked, w_gap, w_fix, hot,
    halo_send, halo_recv, init_send, init_recv, part_send, part_recv,
):
    n_grp, n_dom, planes, ny, nz, n_if = dims
    g, d = lax.axis_index("grp"), lax.axis_index("dom")
    n_dev = n_grp * n_dom
    me = g * n_dom + d
    n_pair = ny // WINDOW

    barrier = pltpu.get_barrier_semaphore()

    def greet(k, carry):
        to = lax.rem(me + k, n_dev)
        pl.semaphore_signal(
            barrier, inc=1, device_id=(to // n_dom, lax.rem(to, n_dom)), device_id_type=MESH
        )
        return carry

    lax.fori_loop(1, n_dev, greet, 0)

    def split_store(x, plane, comp):
        for e in (0, 1):
            y = x if e == 0 else pltpu.roll(x, nz - 1, 1)
            high, low = halves(y)
            turned = jnp.concatenate([y[BLOCK:], y[:BLOCK]], 0)
            high2, low2 = halves(turned)
            at = pl.ds(plane * IN_HALF + (comp * 2 + e) * WINDOW, WINDOW)
            for p in range(n_pair):
                cut = slice(p * WINDOW, (p + 1) * WINDOW)
                split_hi[p, at, :nz] = high[cut]
                split_hi[p, at, nz:] = high2[cut]
                split_lo[p, at, :nz] = low[cut]
                split_lo[p, at, nz:] = low2[cut]

    norm_own[...] = jnp.zeros_like(norm_own)
    norm_own[0:3, 0:n_if] = norm[...]
    o_u[...] = disp[...]
    o_v[...] = vel[...]
    minv[...] = 1.0 / mass[...]

    @pl.when(d == 0)
    def _():
        scale_low[...] = jnp.zeros_like(scale_low)
        for slot in (0, 1):
            halo[slot, 0] = jnp.zeros((3, ny, nz), F32)

    @pl.when(d == n_dom - 1)
    def _():
        for slot in (0, 1):
            halo[slot, 1] = jnp.zeros((3, ny, nz), F32)

    def to_prev(src, slot):
        return pltpu.make_async_remote_copy(
            src_ref=src.at[:, pl.ds(0, ny), :],
            dst_ref=halo.at[slot, 1],
            send_sem=halo_send.at[0],
            recv_sem=halo_recv.at[slot, 1],
            device_id=(g, d - 1),
            device_id_type=MESH,
        )

    def to_next(src, slot):
        return pltpu.make_async_remote_copy(
            src_ref=src.at[:, pl.ds((planes - 1) * ny, ny), :],
            dst_ref=halo.at[slot, 0],
            send_sem=halo_send.at[1],
            recv_sem=halo_recv.at[slot, 0],
            device_id=(g, d + 1),
            device_id_type=MESH,
        )

    scale_copy = pltpu.make_async_remote_copy(
        src_ref=scale.at[pl.ds((planes - 1) * ny, ny), :],
        dst_ref=scale_low,
        send_sem=init_send.at[0],
        recv_sem=init_recv.at[0],
        device_id=(g, d + 1),
        device_id_type=MESH,
    )
    later = (lax.rem(g + 1, n_grp), d)
    norm_copy = pltpu.make_async_remote_copy(
        src_ref=norm_own,
        dst_ref=norm_prev,
        send_sem=init_send.at[1],
        recv_sem=init_recv.at[1],
        device_id=later,
        device_id_type=MESH,
    )
    schur_copy = pltpu.make_async_remote_copy(
        src_ref=schur,
        dst_ref=schur_prev,
        send_sem=init_send.at[2],
        recv_sem=init_recv.at[2],
        device_id=later,
        device_id_type=MESH,
    )

    pl.semaphore_wait(barrier, n_dev - 1)

    @pl.when(d > 0)
    def _():
        to_prev(o_u, 0).start()

    @pl.when(d < n_dom - 1)
    def _():
        to_next(o_u, 0).start()
        scale_copy.start()

    norm_copy.start()
    schur_copy.start()

    high, low = halves(block_matrix(stiff[...]))
    amat[:, 0 : 2 * IN_HALF] = high
    amat[:, 2 * IN_HALF : 4 * IN_HALF] = high
    amat[:, 4 * IN_HALF : 6 * IN_HALF] = low
    for plane in range(planes):
        for comp in range(3):
            split_store(disp[comp, plane * ny : (plane + 1) * ny, :], plane + 1, comp)

    two = 2 * n_if
    nodes = [own[0, i] for i in range(n_if)] + [peer[0, i] for i in range(n_if)]
    node_rows = [node // nz for node in nodes]

    def layer(index, corners, seen):
        first = min(corners) * OUT_HALF
        weights = amat[first : first + len(corners) * OUT_HALF, :]
        for p in range(n_pair):
            rows_in = pl.ds(index * IN_HALF, 2 * IN_HALF)
            top = split_hi[p, rows_in, :]
            stacked = jnp.concatenate([top, split_lo[p, rows_in, :], top], 0)
            result = jnp.dot(weights, stacked, preferred_element_type=F32)
            for half in (0, 1):
                start = (2 * p + half) * BLOCK
                if index == 0:
                    factor = scale_low[start : start + BLOCK, :]
                else:
                    at = (index - 1) * ny + start
                    factor = scale[at : at + BLOCK, :]
                lanes = slice(half * nz, (half + 1) * nz)
                for k, a in enumerate(corners):
                    plane = index - 1 + a
                    for b in (0, 1):
                        for comp in range(3):
                            base = k * OUT_HALF + b * (OUT_HALF // 2) + comp * WINDOW
                            near = result[base : base + BLOCK, lanes] * factor
                            far = result[base + BLOCK : base + WINDOW, lanes] * factor
                            part = near + pltpu.roll(far, 1, 1)
                            at = pl.ds(plane * ny + start, BLOCK)
                            if plane in seen:
                                part = part + force[b, comp, at, :]
                            force[b, comp, at, :] = part
        for a in corners:
            seen.add(index - 1 + a)

    count = jnp.full((1, nz), sub[0], jnp.int32)
    full_delta = coarse_step / count.astype(F32)

    def prepare():
        norm_copy.wait_recv()
        schur_copy.wait_recv()
        lane = iota((two, nz), 1)
        row = iota((two, nz), 0)
        columns = jnp.zeros((two, nz), jnp.int32)
        wide = iota((1, 3 * two), 1)
        rows = jnp.zeros((1, 3 * two), jnp.int32)
        for i in range(two):
            columns = jnp.where(row == i, nodes[i] - node_rows[i] * nz, columns)
            for rep in range(3):
                rows = jnp.where(wide == rep * two + i, node_rows[i], rows)
            picked[0, i : i + 1, :] = minv[pl.ds(node_rows[i], 1), :]
        at_node = lane == columns
        size = planes * ny
        hot[...] = (iota((size, 3 * two), 0) == rows).astype(F32).astype(BF16)
        inverse = picked[0]
        diagonal = iota((n_if, nz), 0) == iota((n_if, nz), 1)
        sign = jnp.where(row < n_if, -1.0, 1.0).astype(F32)
        for comp in range(3):
            cols = []
            for ref in (norm_own, norm_prev):
                spread = jnp.where(diagonal, ref[comp : comp + 1, :], 0.0)
                cols.append(jnp.sum(spread, axis=1, keepdims=True))
            here = jnp.where(at_node, jnp.concatenate(cols, 0), 0.0)
            w_gap[comp] = here
            w_fix[comp] = here * sign * inverse

    def advance(step, carry):
        slot = lax.rem(step, 2)
        seen = set()
        for index in range(1, planes):
            layer(index, (0, 1), seen)

        @pl.when(d > 0)
        def _():
            to_next(o_u, slot).wait_recv()

        @pl.when(d < n_dom - 1)
        def _():
            to_prev(o_u, slot).wait_recv()

        @pl.when((step == 0) & (d > 0))
        def _():
            scale_copy.wait_recv()

        for comp in range(3):
            split_store(halo[slot, 0, comp], 0, comp)
            split_store(halo[slot, 1, comp], planes + 1, comp)
        layer(0, (1,), seen)
        layer(planes, (0,), seen)

        @pl.when(d > 0)
        def _():
            to_prev(o_u, slot).wait_send()

        @pl.when(d < n_dom - 1)
        def _():
            to_next(o_u, slot).wait_send()

        delta = jnp.where(step < count, full_delta, 0.0)
        for plane in range(planes):
            at = slice(plane * ny, (plane + 1) * ny)
            for comp in range(3):
                inner = force[0, comp, at, :] + pltpu.roll(force[1, comp, at, :], 1, 0)
                speed = o_v[comp, at, :] + delta * ((ext[comp, at, :] - inner) * minv[at, :])
                field = o_u[comp, at, :] + delta * speed
                o_v[comp, at, :] = speed
                o_u[comp, at, :] = field
                split_store(field, plane + 1, comp)

        @pl.when((step < MAXSUB - 1) & (d > 0))
        def _():
            to_prev(o_u, 1 - slot).start()

        @pl.when((step < MAXSUB - 1) & (d < n_dom - 1))
        def _():
            to_next(o_u, 1 - slot).start()

        @pl.when(step == 0)
        def _():
            prepare()

        return carry

    lax.fori_loop(0, MAXSUB, advance, 0)

    for comp in range(3):
        for i in range(two):
            picked[comp, i : i + 1, :] = o_v[comp, pl.ds(node_rows[i], 1), :]
    summed = picked[0] * w_gap[0] + picked[1] * w_gap[1] + picked[2] * w_gap[2]
    columns = jnp.sum(summed, axis=1, keepdims=True)
    per_row = nz // n_if
    offset = lax.rem(d, per_row) * n_if
    place = iota((n_if, nz), 1) == iota((n_if, nz), 0) + offset
    for k in (0, 1):
        spread = jnp.where(place, columns[k * n_if : (k + 1) * n_if, :], 0.0)
        parts[me, k : k + 1, :] = jnp.sum(spread, axis=0, keepdims=True)

    def part_copy(to, source):
        return pltpu.make_async_remote_copy(
            src_ref=parts.at[source],
            dst_ref=parts.at[source],
            send_sem=part_send.at[to],
            recv_sem=part_recv.at[source],
            device_id=(to // n_dom, lax.rem(to, n_dom)),
            device_id_type=MESH,
        )

    def send(k, carry):
        part_copy(lax.rem(me + k, n_dev), me).start()
        return carry

    def receive(k, carry):
        source = lax.rem(me + k, n_dev)
        part_copy(source, source).wait_recv()
        return carry

    def finish(k, carry):
        part_copy(lax.rem(me + k, n_dev), me).wait_send()
        return carry

    lax.fori_loop(1, n_dev, send, 0)
    lax.fori_loop(1, n_dev, receive, 0)

    n_rows = n_dom // per_row
    totals = [
        [
            jnp.sum(parts[group * n_dom + k * per_row : group * n_dom + (k + 1) * per_row], axis=0)
            for k in range(n_rows)
        ]
        for group in range(n_grp)
    ]
    mine = jnp.zeros((n_if, nz), F32)
    before = jnp.zeros((n_if, nz), F32)
    for group in range(n_grp):
        for k in range(n_rows):
            gap = totals[group][k][0:1] - totals[(group + 1) % n_grp][k][1:2]
            at = slice((group * n_rows + k) * nz, (group * n_rows + k + 1) * nz)
            mine = mine + schur[:, at] * gap
            before = before + schur_prev[:, at] * gap
    factors = jnp.sum(jnp.concatenate([mine, before], 0), axis=1, keepdims=True)
    fixes = jnp.concatenate([factors * w_fix[comp] for comp in range(3)], 1)
    first, rest = fixes.astype(BF16), fixes
    rest = rest - first.astype(F32)
    second = rest.astype(BF16)
    third = (rest - second.astype(F32)).astype(BF16)
    change = jnp.dot(
        hot[...], jnp.concatenate([first, second, third], 0), preferred_element_type=F32
    )
    for comp in range(3):
        o_v[comp] = o_v[comp] + change[:, comp * nz : (comp + 1) * nz]

    lax.fori_loop(1, n_dev, finish, 0)
    norm_copy.wait_send()
    schur_copy.wait_send()

    @pl.when(d < n_dom - 1)
    def _():
        scale_copy.wait_send()


def solution(mesh):
    n_grp, n_dom = mesh.shape["grp"], mesh.shape["dom"]

    def on_device(
        displacement, velocity, external, mass, elem_scale, stiffness,
        substeps, own_nodes, peer_nodes, normals, schur_inverse,
    ):
        _, _, planes, ny, nz = displacement.shape
        n_if = own_nodes.shape[1]
        n_dev = n_grp * n_dom
        n_lam = schur_inverse.shape[1]
        rows = planes * ny
        field = jax.ShapeDtypeStruct((3, rows, nz), F32)
        vmem = pl.BlockSpec(memory_space=pltpu.VMEM)
        smem = pl.BlockSpec(memory_space=pltpu.SMEM)
        new_u, new_v = pl.pallas_call(
            functools.partial(kernel, (n_grp, n_dom, planes, ny, nz, n_if)),
            out_shape=(field, field),
            in_specs=[vmem] * 6 + [smem] * 3 + [vmem] * 2,
            out_specs=(vmem, vmem),
            scratch_shapes=[
                pltpu.VMEM((ny // WINDOW, (planes + 2) * IN_HALF, 2 * nz), BF16),
                pltpu.VMEM((ny // WINDOW, (planes + 2) * IN_HALF, 2 * nz), BF16),
                pltpu.VMEM((2, 3, rows, nz), F32),
                pltpu.VMEM((2, 2, 3, ny, nz), F32),
                pltpu.VMEM((ny, nz), F32),
                pltpu.VMEM((rows, nz), F32),
                pltpu.VMEM((2 * OUT_HALF, 6 * IN_HALF), BF16),
                pltpu.VMEM((8, nz), F32),
                pltpu.VMEM((8, nz), F32),
                pltpu.VMEM((n_if, n_lam), F32),
                pltpu.VMEM((n_dev, 2, nz), F32),
                pltpu.VMEM((3, 2 * n_if, nz), F32),
                pltpu.VMEM((3, 2 * n_if, nz), F32),
                pltpu.VMEM((3, 2 * n_if, nz), F32),
                pltpu.VMEM((rows, 6 * n_if), BF16),
                pltpu.SemaphoreType.DMA((2,)),
                pltpu.SemaphoreType.DMA((2, 2)),
                pltpu.SemaphoreType.DMA((3,)),
                pltpu.SemaphoreType.DMA((3,)),
                pltpu.SemaphoreType.DMA((n_dev,)),
                pltpu.SemaphoreType.DMA((n_dev,)),
            ],
            compiler_params=pltpu.CompilerParams(
                collective_id=0, has_side_effects=True, vmem_limit_bytes=48 << 20
            ),
        )(
            displacement.reshape(3, rows, nz),
            velocity.reshape(3, rows, nz),
            external.reshape(3, rows, nz),
            mass.reshape(rows, nz),
            elem_scale.reshape(rows, nz),
            stiffness[0],
            substeps,
            own_nodes,
            peer_nodes,
            normals[0],
            schur_inverse,
        )
        shape = displacement.shape
        return new_u.reshape(shape), new_v.reshape(shape)

    return jax.shard_map(
        on_device,
        mesh=mesh,
        in_specs=(
            P("grp", None, "dom", None, None),
            P("grp", None, "dom", None, None),
            P("grp", None, "dom", None, None),
            P("grp", "dom", None, None),
            P("grp", "dom", None, None),
            P("grp", None, None),
            P("grp"),
            P("grp", "dom"),
            P("grp", "dom"),
            P("grp", None, "dom"),
            P(("grp", "dom"), None),
        ),
        out_specs=(P("grp", None, "dom", None, None), P("grp", None, "dom", None, None)),
        check_vma=False,
    )
```

time: 272 us -> 62.5 us (0.23)
  other arithmetic: 68.5 us -> 0 us
  starting transfers between devices: 62.8 us -> 0 us
  local copies, waits for them, and re-layouts: 67.4 us -> 8.21 us
  Pallas kernels: 0 us -> 52.6 us
  blocking collectives: 42.1 us -> 0 us
  matrix products: 17.7 us -> 0 us
  loops' own time: 7.78 us -> 0 us
    ppermute x18 -> x0, starting transfers between devices: 62.8 us -> none  [the longest x16 58 us: shifted(): return lax.ppermute(x, axis, pairs)]
    pallas_call x0 -> x1, Pallas kernels: none -> 52.6 us  [on_device(): pl.pallas_call(functools.partial(kernel, (n_grp, n_dom, planes, ny, nz, n...]
    unnamed x1 -> x0, blocking collectives: 42.1 us -> none
    while x40 -> x0, other arithmetic: 32.4 us -> none
    while x161 -> x0, local copies, waits for them, and re-layouts: 24.4 us -> none
    scatter-add x2 -> x0, other arithmetic: 19.4 us -> none  [the longest x1 9.72 us: on_device(): flat_speed = flat_speed.at[:, peer].add(incoming / masses[peer][None, :])]
    dot_general x9 -> x0, matrix products: 17.7 us -> none  [the longest x8 17.6 us: element_forces(): jnp.dot(kmat, stacked, precision=lax.Precision.HIGHEST, preferred_element...]
    reshape x8 -> x0, local copies, waits for them, and re-layouts: 15.3 us -> none  [corner_stack(): return jnp.stack(pieces, 0).reshape(24, -1)]
  transfers between devices with their start and end apart: 18 -> 0, of which waited for: 8 -> 0; matrix products, arithmetic and copies ran while one was open for 17% -> 0% of each run, Pallas kernels for 0% -> 0%
where the time goes in v1:
time: 62.5 us; the launch traced here: 62.1 us
  Pallas kernels  52.6 us (84%)
  local copies, waits for them, and re-layouts  8.21 us (13%)
  between operations  1.32 us (2%)
    pallas_call x1, Pallas kernels, on_device(): pl.pallas_call(functools.partial(kernel, (n_grp, n_dom, planes, ny, nz, n...  52.6 us
    unnamed x21, local copies, waits for them, and re-layouts  8.21 us

profile of v1, /device:TPU:0, one launch (start us, length us, event | category | flops | bytes accessed | tf_op | source)
XLA Modules:
  0.0 62.1 jit_solution(11142033793806994275)
XLA Ops:
  0.6 0.0 copy-start.6
  1.3 0.7 %copy.15 = f32[1,3,16]{2,1,0:T(4,128)S(1)} copy(f32[1,3,16]{2,0,1:T(1,128)} %param.20) | data formatting | bytes 384
  2.0 0.0 copy-start.7
  2.0 0.0 copy-start.8
  2.0 0.0 copy-done.6
  2.0 0.6 %copy-done.7 = s32[1,16]{1,0:T(1,128)S(1)} copy-done((s32[1,16]{1,0:T(1,128)S(1)}, s32[1,16]{1,0:T(1,128)}, u32[]{:S(2)}) %copy-start.7) | copy-done | bytes 88
  2.6 0.0 copy-done.8
  2.7 0.0 copy-start
  2.7 1.0 %copy-done = f32[1,3,2,96,128]{4,3,2,1,0:T(8,128)S(1)} copy-done((f32[1,3,2,96,128]{4,3,2,1,0:T(8,128)S(1)}, f32[1,3,2,96,128]{4,3,2,1,0:T(8,128)}, u32[]{:S(2)}) %copy-start) | copy-done | bytes 294936
  3.6 0.0 copy-start.1
  3.6 1.0 %copy-done.1 = f32[1,3,2,96,128]{4,3,2,1,0:T(8,128)S(1)} copy-done((f32[1,3,2,96,128]{4,3,2,1,0:T(8,128)S(1)}, f32[1,3,2,96,128]{4,3,2,1,0:T(8,128)}, u32[]{:S(2)}) %copy-start.1) | copy-done | bytes 294936
  4.6 0.0 copy-start.2
  4.6 1.0 %copy-done.2 = f32[1,3,2,96,128]{4,3,2,1,0:T(8,128)S(1)} copy-done((f32[1,3,2,96,128]{4,3,2,1,0:T(8,128)S(1)}, f32[1,3,2,96,128]{4,3,2,1,0:T(8,128)}, u32[]{:S(2)}) %copy-start.2) | copy-done | bytes 294936
  5.5 0.0 copy-start.3
  5.5 0.9 %copy-done.3 = f32[1,2,96,128]{3,2,1,0:T(8,128)S(1)} copy-done((f32[1,2,96,128]{3,2,1,0:T(8,128)S(1)}, f32[1,2,96,128]{3,2,1,0:T(8,128)}, u32[]{:S(2)}) %copy-start.3) | copy-done | bytes 98328
  6.4 0.0 copy-start.4
  6.4 0.9 %copy-done.4 = f32[1,2,96,128]{3,2,1,0:T(8,128)S(1)} copy-done((f32[1,2,96,128]{3,2,1,0:T(8,128)S(1)}, f32[1,2,96,128]{3,2,1,0:T(8,128)}, u32[]{:S(2)}) %copy-start.4) | copy-done | bytes 98328
  7.3 0.0 copy-start.5
  7.3 0.8 %copy-done.5 = f32[16,512]{1,0:T(8,128)S(1)} copy-done((f32[16,512]{1,0:T(8,128)S(1)}, f32[16,512]{1,0:T(8,128)}, u32[]{:S(2)}) %copy-start.5) | copy-done | bytes 32792
  8.1 52.6 %shard_map.122 = (f32[3,192,128]{2,1,0:T(8,128)S(1)}, f32[3,192,128]{2,1,0:T(8,128)S(1)}) custom-call(f32[3,192,128]{2,1,0:T(8,128)S(1)} %bitcast.11, f32[3,192,128]{2,1,0:T(8,128)S(1)} %bitcast.12, f32[3,192,128]{2,1,0:T(8,128)S(1)} %bitcast.13, f32[192,128]{1,0:T(8,128)S(1)} %bitcast.16, f32[192,128]{1,0:T(8,128)S(1)} %bitcast.17, f32[24,24]{1,0:T(8,128)S(1)} %bitcast.18, ...), custom_call_target="tpu_custom_call" | custom-call | tf_op jit(solution)/shard_map/pallas_call | solution.py:400
  60.7 0.7 %copy.19 = f32[1,3,2,96,128]{4,3,2,1,0:T(8,128)} copy(f32[1,3,2,96,128]{4,3,2,1,0:T(8,128)S(1)} %bitcast.15) | data formatting | bytes 589824
  61.4 0.7 %copy.20 = f32[1,3,2,96,128]{4,3,2,1,0:T(8,128)} copy(f32[1,3,2,96,128]{4,3,2,1,0:T(8,128)S(1)} %bitcast.14) | data formatting | bytes 589824
Async XLA Ops:
  0.6 1.4 %copy-start.6 = (f32[1,24,24]{2,1,0:T(8,128)S(1)}, f32[1,24,24]{2,1,0:T(8,128)}, u32[]{:S(2)}) copy-start(f32[1,24,24]{2,1,0:T(8,128)} %param.16) | copy-start | bytes 6916
  2.0 0.7 %copy-start.7 = (s32[1,16]{1,0:T(1,128)S(1)}, s32[1,16]{1,0:T(1,128)}, u32[]{:S(2)}) copy-start(s32[1,16]{1,0:T(1,128)} %own.1) | copy-start | bytes 196
  2.0 0.7 %copy-start.8 = (s32[1,16]{1,0:T(1,128)S(1)}, s32[1,16]{1,0:T(1,128)}, u32[]{:S(2)}) copy-start(s32[1,16]{1,0:T(1,128)} %peer.1) | copy-start | bytes 196
  2.7 1.0 %copy-start = (f32[1,3,2,96,128]{4,3,2,1,0:T(8,128)S(1)}, f32[1,3,2,96,128]{4,3,2,1,0:T(8,128)}, u32[]{:S(2)}) copy-start(f32[1,3,2,96,128]{4,3,2,1,0:T(8,128)} %param.11) | copy-start | bytes 884740
  3.6 1.0 %copy-start.1 = (f32[1,3,2,96,128]{4,3,2,1,0:T(8,128)S(1)}, f32[1,3,2,96,128]{4,3,2,1,0:T(8,128)}, u32[]{:S(2)}) copy-start(f32[1,3,2,96,128]{4,3,2,1,0:T(8,128)} %param.12) | copy-start | bytes 884740
  4.6 1.0 %copy-start.2 = (f32[1,3,2,96,128]{4,3,2,1,0:T(8,128)S(1)}, f32[1,3,2,96,128]{4,3,2,1,0:T(8,128)}, u32[]{:S(2)}) copy-start(f32[1,3,2,96,128]{4,3,2,1,0:T(8,128)} %param.13) | copy-start | bytes 884740
  5.5 0.9 %copy-start.3 = (f32[1,2,96,128]{3,2,1,0:T(8,128)S(1)}, f32[1,2,96,128]{3,2,1,0:T(8,128)}, u32[]{:S(2)}) copy-start(f32[1,2,96,128]{3,2,1,0:T(8,128)} %param.14) | copy-start | bytes 294916
  6.4 0.9 %copy-start.4 = (f32[1,2,96,128]{3,2,1,0:T(8,128)S(1)}, f32[1,2,96,128]{3,2,1,0:T(8,128)}, u32[]{:S(2)}) copy-start(f32[1,2,96,128]{3,2,1,0:T(8,128)} %param.15) | copy-start | bytes 294916
  7.3 0.8 %copy-start.5 = (f32[16,512]{1,0:T(8,128)S(1)}, f32[16,512]{1,0:T(8,128)}, u32[]{:S(2)}) copy-start(f32[16,512]{1,0:T(8,128)} %schur.1) | copy-start | bytes 98308

commit v2 on v1

--- a/solution.py
+++ b/solution.py
@@ -60,11 +60,12 @@
 
 
 def kernel(
-    dims, disp, vel, ext, mass, scale, stiff, sub, own, peer, norm, schur,
+    dims, disp, vel, ext_in, mass_in, scale_in, stiff_in, sub_in, own_in, peer_in, norm_in, schur_in,
     o_u, o_v,
+    ext, mass, scale, stiff, sub, own, peer, norm, schur,
     split_hi, split_lo, force, halo, scale_low, minv, amat, norm_own, norm_prev, schur_prev,
     parts, picked, w_gap, w_fix, hot,
-    halo_send, halo_recv, init_send, init_recv, part_send, part_recv,
+    in_sem, halo_send, halo_recv, init_send, init_recv, part_send, part_recv,
 ):
     n_grp, n_dom, planes, ny, nz, n_if = dims
     g, d = lax.axis_index("grp"), lax.axis_index("dom")
@@ -81,27 +82,48 @@
         )
         return carry
 
+    sources = (disp, vel, ext_in, mass_in, scale_in, stiff_in, sub_in, own_in, peer_in, norm_in, schur_in)
+    places = (o_u, o_v, ext, mass, scale, stiff, sub, own, peer, norm, schur)
+    loads = [
+        pltpu.make_async_copy(source, place, in_sem.at[k])
+        for k, (source, place) in enumerate(zip(sources, places))
+    ]
+    for k in (5, 0, 3, 4, 9, 10, 1, 2, 6, 7, 8):
+        loads[k].start()
     lax.fori_loop(1, n_dev, greet, 0)
 
-    def split_store(x, plane, comp):
-        for e in (0, 1):
-            y = x if e == 0 else pltpu.roll(x, nz - 1, 1)
-            high, low = halves(y)
-            turned = jnp.concatenate([y[BLOCK:], y[:BLOCK]], 0)
-            high2, low2 = halves(turned)
-            at = pl.ds(plane * IN_HALF + (comp * 2 + e) * WINDOW, WINDOW)
-            for p in range(n_pair):
-                cut = slice(p * WINDOW, (p + 1) * WINDOW)
-                split_hi[p, at, :nz] = high[cut]
-                split_hi[p, at, nz:] = high2[cut]
-                split_lo[p, at, :nz] = low[cut]
-                split_lo[p, at, nz:] = low2[cut]
-
-    norm_own[...] = jnp.zeros_like(norm_own)
-    norm_own[0:3, 0:n_if] = norm[...]
-    o_u[...] = disp[...]
-    o_v[...] = vel[...]
-    minv[...] = 1.0 / mass[...]
+    def rows_at(start, size):
+        return pl.ds(pl.multiple_of(start, BLOCK), size)
+
+    def after(q):
+        return lax.rem(q + 1, n_pair)
+
+    def before(q):
+        return lax.rem(q + n_pair - 1, n_pair)
+
+    def split_window(load, plane, q, odd):
+        for comp in range(3):
+            if odd:
+                x = jnp.concatenate(
+                    [load(comp, q * WINDOW + BLOCK), load(comp, after(q) * WINDOW)], 0
+                )
+            else:
+                x = jnp.concatenate(
+                    [load(comp, q * WINDOW), load(comp, q * WINDOW + BLOCK)], 0
+                )
+            for e in (0, 1):
+                y = x if e == 0 else pltpu.roll(x, nz - 1, 1)
+                high, low = halves(y)
+                at = pl.ds(plane * IN_HALF + (comp * 2 + e) * WINDOW, WINDOW)
+                lanes = slice(nz, 2 * nz) if odd else slice(0, nz)
+                split_hi[q, at, lanes] = high
+                split_lo[q, at, lanes] = low
+
+    def own_rows(plane):
+        return lambda comp, start: o_u[comp, rows_at(plane * ny + start, BLOCK), :]
+
+    def halo_rows(slot, side):
+        return lambda comp, start: halo[slot, side, comp, rows_at(start, BLOCK), :]
 
     @pl.when(d == 0)
     def _():
@@ -114,22 +136,22 @@
         for slot in (0, 1):
             halo[slot, 1] = jnp.zeros((3, ny, nz), F32)
 
-    def to_prev(src, slot):
+    def to_prev(slot, q):
         return pltpu.make_async_remote_copy(
-            src_ref=src.at[:, pl.ds(0, ny), :],
-            dst_ref=halo.at[slot, 1],
-            send_sem=halo_send.at[0],
-            recv_sem=halo_recv.at[slot, 1],
+            src_ref=o_u.at[:, rows_at(q * WINDOW, WINDOW), :],
+            dst_ref=halo.at[slot, 1, :, rows_at(q * WINDOW, WINDOW), :],
+            send_sem=halo_send.at[0, q],
+            recv_sem=halo_recv.at[slot, 1, q],
             device_id=(g, d - 1),
             device_id_type=MESH,
         )
 
-    def to_next(src, slot):
+    def to_next(slot, q):
         return pltpu.make_async_remote_copy(
-            src_ref=src.at[:, pl.ds((planes - 1) * ny, ny), :],
-            dst_ref=halo.at[slot, 0],
-            send_sem=halo_send.at[1],
-            recv_sem=halo_recv.at[slot, 0],
+            src_ref=o_u.at[:, rows_at((planes - 1) * ny + q * WINDOW, WINDOW), :],
+            dst_ref=halo.at[slot, 0, :, rows_at(q * WINDOW, WINDOW), :],
+            send_sem=halo_send.at[1, q],
+            recv_sem=halo_recv.at[slot, 0, q],
             device_id=(g, d + 1),
             device_id_type=MESH,
         )
@@ -160,62 +182,65 @@
         device_id_type=MESH,
     )
 
-    pl.semaphore_wait(barrier, n_dev - 1)
-
-    @pl.when(d > 0)
-    def _():
-        to_prev(o_u, 0).start()
-
-    @pl.when(d < n_dom - 1)
-    def _():
-        to_next(o_u, 0).start()
-        scale_copy.start()
-
-    norm_copy.start()
-    schur_copy.start()
-
+    loads[5].wait()
     high, low = halves(block_matrix(stiff[...]))
     amat[:, 0 : 2 * IN_HALF] = high
     amat[:, 2 * IN_HALF : 4 * IN_HALF] = high
     amat[:, 4 * IN_HALF : 6 * IN_HALF] = low
+    for k in (0, 1, 2, 3, 4, 6, 7, 8, 9, 10):
+        loads[k].wait()
+    norm_own[...] = jnp.zeros_like(norm_own)
+    for comp in range(3):
+        norm_own[comp : comp + 1, 0:n_if] = norm[comp]
+    minv[...] = 1.0 / mass[...]
     for plane in range(planes):
-        for comp in range(3):
-            split_store(disp[comp, plane * ny : (plane + 1) * ny, :], plane + 1, comp)
+        for q in range(n_pair):
+            for odd in (False, True):
+                split_window(own_rows(plane), plane + 1, jnp.int32(q), odd)
+
+    pl.semaphore_wait(barrier, n_dev - 1)
+
+    for q in range(n_pair):
+        @pl.when(d > 0)
+        def _():
+            to_prev(0, q).start()
+
+        @pl.when(d < n_dom - 1)
+        def _():
+            to_next(0, q).start()
+            if q == 1:
+                scale_copy.start()
+
+    norm_copy.start()
+    schur_copy.start()
 
     two = 2 * n_if
     nodes = [own[0, i] for i in range(n_if)] + [peer[0, i] for i in range(n_if)]
     node_rows = [node // nz for node in nodes]
 
-    def layer(index, corners, seen):
+    def layer(index, corners, q, total):
         first = min(corners) * OUT_HALF
         weights = amat[first : first + len(corners) * OUT_HALF, :]
-        for p in range(n_pair):
-            rows_in = pl.ds(index * IN_HALF, 2 * IN_HALF)
-            top = split_hi[p, rows_in, :]
-            stacked = jnp.concatenate([top, split_lo[p, rows_in, :], top], 0)
-            result = jnp.dot(weights, stacked, preferred_element_type=F32)
-            for half in (0, 1):
-                start = (2 * p + half) * BLOCK
-                if index == 0:
-                    factor = scale_low[start : start + BLOCK, :]
-                else:
-                    at = (index - 1) * ny + start
-                    factor = scale[at : at + BLOCK, :]
-                lanes = slice(half * nz, (half + 1) * nz)
-                for k, a in enumerate(corners):
-                    plane = index - 1 + a
-                    for b in (0, 1):
-                        for comp in range(3):
-                            base = k * OUT_HALF + b * (OUT_HALF // 2) + comp * WINDOW
-                            near = result[base : base + BLOCK, lanes] * factor
-                            far = result[base + BLOCK : base + WINDOW, lanes] * factor
-                            part = near + pltpu.roll(far, 1, 1)
-                            at = pl.ds(plane * ny + start, BLOCK)
-                            if plane in seen:
-                                part = part + force[b, comp, at, :]
-                            force[b, comp, at, :] = part
-        for a in corners:
-            seen.add(index - 1 + a)
+        rows_in = pl.ds(index * IN_HALF, 2 * IN_HALF)
+        top = split_hi[q, rows_in, :]
+        stacked = jnp.concatenate([top, split_lo[q, rows_in, :], top], 0)
+        result = jnp.dot(weights, stacked, preferred_element_type=F32)
+        for half in (0, 1):
+            start = q * WINDOW + half * BLOCK
+            if index == 0:
+                factor = scale_low[rows_at(start, BLOCK), :]
+            else:
+                factor = scale[rows_at((index - 1) * ny + start, BLOCK), :]
+            lanes = slice(half * nz, (half + 1) * nz)
+            for k, a in enumerate(corners):
+                for b in (0, 1):
+                    for comp in range(3):
+                        base = k * OUT_HALF + b * (OUT_HALF // 2) + comp * WINDOW
+                        near = result[base : base + BLOCK, lanes] * factor
+                        far = result[base + BLOCK : base + WINDOW, lanes] * factor
+                        part = near + pltpu.roll(far, 1, 1)
+                        key = (index - 1 + a, b, comp, half)
+                        total[key] = total[key] + part if key in total else part
 
     count = jnp.full((1, nz), sub[0], jnp.int32)
     full_delta = coarse_step / count.astype(F32)
@@ -250,54 +275,83 @@
 
     def advance(step, carry):
         slot = lax.rem(step, 2)
-        seen = set()
-        for index in range(1, planes):
-            layer(index, (0, 1), seen)
-
-        @pl.when(d > 0)
-        def _():
-            to_next(o_u, slot).wait_recv()
-
-        @pl.when(d < n_dom - 1)
-        def _():
-            to_prev(o_u, slot).wait_recv()
-
-        @pl.when((step == 0) & (d > 0))
-        def _():
-            scale_copy.wait_recv()
-
-        for comp in range(3):
-            split_store(halo[slot, 0, comp], 0, comp)
-            split_store(halo[slot, 1, comp], planes + 1, comp)
-        layer(0, (1,), seen)
-        layer(planes, (0,), seen)
-
-        @pl.when(d > 0)
-        def _():
-            to_prev(o_u, slot).wait_send()
-
-        @pl.when(d < n_dom - 1)
-        def _():
-            to_next(o_u, slot).wait_send()
-
         delta = jnp.where(step < count, full_delta, 0.0)
-        for plane in range(planes):
-            at = slice(plane * ny, (plane + 1) * ny)
-            for comp in range(3):
-                inner = force[0, comp, at, :] + pltpu.roll(force[1, comp, at, :], 1, 0)
-                speed = o_v[comp, at, :] + delta * ((ext[comp, at, :] - inner) * minv[at, :])
-                field = o_u[comp, at, :] + delta * speed
-                o_v[comp, at, :] = speed
-                o_u[comp, at, :] = field
-                split_store(field, plane + 1, comp)
-
-        @pl.when((step < MAXSUB - 1) & (d > 0))
-        def _():
-            to_prev(o_u, 1 - slot).start()
-
-        @pl.when((step < MAXSUB - 1) & (d < n_dom - 1))
-        def _():
-            to_next(o_u, 1 - slot).start()
+        order = [lax.rem(step + i, n_pair) for i in range(n_pair)]
+
+        def arrive(q):
+            @pl.when(d > 0)
+            def _():
+                to_next(slot, q).wait_recv()
+
+            @pl.when(d < n_dom - 1)
+            def _():
+                to_prev(slot, q).wait_recv()
+
+        def update(q):
+            @pl.when(d > 0)
+            def _():
+                to_prev(slot, q).wait_send()
+
+            @pl.when(d < n_dom - 1)
+            def _():
+                to_next(slot, q).wait_send()
+
+            for plane in range(planes):
+                at = rows_at(plane * ny + q * WINDOW, WINDOW)
+                last = rows_at(plane * ny + before(q) * WINDOW + BLOCK, BLOCK)
+                for comp in range(3):
+                    shifted = jnp.concatenate([force[1, comp, last, :], force[1, comp, at, :]], 0)
+                    shifted = pltpu.roll(shifted, 1, 0)[BLOCK:]
+                    inner = force[0, comp, at, :] + shifted
+                    speed = o_v[comp, at, :] + delta * ((ext[comp, at, :] - inner) * minv[at, :])
+                    o_v[comp, at, :] = speed
+                    o_u[comp, at, :] = o_u[comp, at, :] + delta * speed
+
+            @pl.when((step < MAXSUB - 1) & (d > 0))
+            def _():
+                to_prev(1 - slot, q).start()
+
+            @pl.when((step < MAXSUB - 1) & (d < n_dom - 1))
+            def _():
+                to_next(1 - slot, q).start()
+
+        def own_windows(q, odd):
+            for plane in range(planes):
+                split_window(own_rows(plane), plane + 1, q, odd)
+
+        def halo_windows(q, odd):
+            split_window(halo_rows(slot, 0), 0, q, odd)
+            split_window(halo_rows(slot, 1), planes + 1, q, odd)
+
+        for i, q in enumerate(order):
+            total = {}
+            for index in range(1, planes):
+                layer(index, (0, 1), q, total)
+            if i == 0:
+                @pl.when((step == 0) & (d > 0))
+                def _():
+                    scale_copy.wait_recv()
+
+                arrive(q)
+                halo_windows(q, False)
+            if i < n_pair - 1:
+                arrive(order[i + 1])
+                halo_windows(order[i + 1], False)
+            halo_windows(q, True)
+            layer(0, (1,), q, total)
+            layer(planes, (0,), q, total)
+            for (plane, b, comp, half), part in total.items():
+                at = rows_at(plane * ny + q * WINDOW + half * BLOCK, BLOCK)
+                force[b, comp, at, :] = part
+            if i > 0:
+                update(q)
+                own_windows(q, False)
+            if i > 1:
+                own_windows(order[i - 1], True)
+        update(order[0])
+        own_windows(order[0], False)
+        own_windows(order[0], True)
+        own_windows(order[-1], True)
 
         @pl.when(step == 0)
         def _():
@@ -396,13 +450,21 @@
         rows = planes * ny
         field = jax.ShapeDtypeStruct((3, rows, nz), F32)
         vmem = pl.BlockSpec(memory_space=pltpu.VMEM)
-        smem = pl.BlockSpec(memory_space=pltpu.SMEM)
         new_u, new_v = pl.pallas_call(
             functools.partial(kernel, (n_grp, n_dom, planes, ny, nz, n_if)),
             out_shape=(field, field),
-            in_specs=[vmem] * 6 + [smem] * 3 + [vmem] * 2,
+            in_specs=[pl.BlockSpec(memory_space=pltpu.HBM)] * 11,
             out_specs=(vmem, vmem),
             scratch_shapes=[
+                pltpu.VMEM((3, rows, nz), F32),
+                pltpu.VMEM((rows, nz), F32),
+                pltpu.VMEM((rows, nz), F32),
+                pltpu.VMEM((24, 24), F32),
+                pltpu.SMEM((1,), jnp.int32),
+                pltpu.SMEM((1, n_if), jnp.int32),
+                pltpu.SMEM((1, n_if), jnp.int32),
+                pltpu.VMEM((3, 1, n_if), F32),
+                pltpu.VMEM((n_if, n_lam), F32),
                 pltpu.VMEM((ny // WINDOW, (planes + 2) * IN_HALF, 2 * nz), BF16),
                 pltpu.VMEM((ny // WINDOW, (planes + 2) * IN_HALF, 2 * nz), BF16),
                 pltpu.VMEM((2, 3, rows, nz), F32),
@@ -418,15 +480,16 @@
                 pltpu.VMEM((3, 2 * n_if, nz), F32),
                 pltpu.VMEM((3, 2 * n_if, nz), F32),
                 pltpu.VMEM((rows, 6 * n_if), BF16),
-                pltpu.SemaphoreType.DMA((2,)),
-                pltpu.SemaphoreType.DMA((2, 2)),
+                pltpu.SemaphoreType.DMA((11,)),
+                pltpu.SemaphoreType.DMA((2, ny // WINDOW)),
+                pltpu.SemaphoreType.DMA((2, 2, ny // WINDOW)),
                 pltpu.SemaphoreType.DMA((3,)),
                 pltpu.SemaphoreType.DMA((3,)),
                 pltpu.SemaphoreType.DMA((n_dev,)),
                 pltpu.SemaphoreType.DMA((n_dev,)),
             ],
             compiler_params=pltpu.CompilerParams(
-                collective_id=0, has_side_effects=True, vmem_limit_bytes=48 << 20
+                collective_id=0, has_side_effects=True, vmem_limit_bytes=67_043_328
             ),
         )(
             displacement.reshape(3, rows, nz),
@@ -438,7 +501,7 @@
             substeps,
             own_nodes,
             peer_nodes,
-            normals[0],
+            jnp.transpose(normals, (1, 0, 2)),
             schur_inverse,
         )
         shape = displacement.shape

time: 62.5 us -> 61.6 us (0.986)
  local copies, waits for them, and re-layouts: 8.21 us -> 2.46 us
  Pallas kernels: 52.6 us -> 57.7 us
    unnamed x21 -> x4, local copies, waits for them, and re-layouts: 8.21 us -> 2.46 us
    pallas_call x1, Pallas kernels: 52.6 us -> 57.7 us  [on_device(): pl.pallas_call(functools.partial(kernel, (n_grp, n_dom, planes, ny, nz, n...]
where the time goes in v2:
time: 61.6 us; the launch traced here: 61.4 us
  Pallas kernels  57.7 us (94%)
  local copies, waits for them, and re-layouts  2.46 us (4%)
  between operations  1.3 us (2%)
    pallas_call x1, Pallas kernels, on_device(): pl.pallas_call(functools.partial(kernel, (n_grp, n_dom, planes, ny, nz, n...  57.7 us
    unnamed x4, local copies, waits for them, and re-layouts  2.46 us

profile of v2, /device:TPU:0, one launch (start us, length us, event | category | flops | bytes accessed | tf_op | source)
XLA Modules:
  0.0 61.4 jit_solution(4201296524565867398)
XLA Ops:
  1.3 57.7 %shard_map.122 = (f32[3,192,128]{2,1,0:T(8,128)}, f32[3,192,128]{2,1,0:T(8,128)}) custom-call(f32[3,192,128]{2,1,0:T(8,128)} %bitcast.9, f32[3,192,128]{2,1,0:T(8,128)} %bitcast.10, f32[3,192,128]{2,1,0:T(8,128)} %bitcast.11, f32[192,128]{1,0:T(8,128)} %bitcast.14, f32[192,128]{1,0:T(8,128)} %bitcast.15, f32[24,24]{1,0:T(8,128)} %bitcast.16, ...), custom_call_target="tpu_custom_call" | custom-call | tf_op jit(solution)/shard_map/pallas_call | solution.py:453
  59.0 0.0 copy-start
  59.0 1.7 %copy.16 = f32[1,3,2,96,128]{4,3,2,1,0:T(8,128)} copy(f32[1,3,2,96,128]{4,3,2,1,0:T(8,128)} %bitcast.13) | data formatting | bytes 589824
  60.7 0.0 copy-done
  60.7 0.7 %copy.17 = f32[1,3,2,96,128]{4,3,2,1,0:T(8,128)} copy(f32[1,3,2,96,128]{4,3,2,1,0:T(8,128)S(1)} %bitcast.12) | data formatting | bytes 589824
Async XLA Ops:
  59.0 1.8 %copy-start = (f32[3,192,128]{2,1,0:T(8,128)S(1)}, f32[3,192,128]{2,1,0:T(8,128)}, u32[]{:S(2)}) copy-start(f32[3,192,128]{2,1,0:T(8,128)} %get-tuple-element.5) | copy-start | bytes 884740

commit v3 on v2

--- a/solution.py
+++ b/solution.py
@@ -8,6 +8,7 @@
 from jax.sharding import PartitionSpec as P
 
 MAXSUB = 8
+TURN = 4
 MESH = pl.DeviceIdType.MESH
 HIGH = lax.Precision.HIGHEST
 F32 = jnp.float32
@@ -93,13 +94,13 @@
     lax.fori_loop(1, n_dev, greet, 0)
 
     def rows_at(start, size):
-        return pl.ds(pl.multiple_of(start, BLOCK), size)
+        return pl.ds(start, size)
 
     def after(q):
-        return lax.rem(q + 1, n_pair)
+        return (q + 1) % n_pair
 
     def before(q):
-        return lax.rem(q + n_pair - 1, n_pair)
+        return (q - 1) % n_pair
 
     def split_window(load, plane, q, odd):
         for comp in range(3):
@@ -196,7 +197,7 @@
     for plane in range(planes):
         for q in range(n_pair):
             for odd in (False, True):
-                split_window(own_rows(plane), plane + 1, jnp.int32(q), odd)
+                split_window(own_rows(plane), plane + 1, q, odd)
 
     pl.semaphore_wait(barrier, n_dev - 1)
 
@@ -218,7 +219,7 @@
     nodes = [own[0, i] for i in range(n_if)] + [peer[0, i] for i in range(n_if)]
     node_rows = [node // nz for node in nodes]
 
-    def layer(index, corners, q, total):
+    def layer(index, corners, q, seen):
         first = min(corners) * OUT_HALF
         weights = amat[first : first + len(corners) * OUT_HALF, :]
         rows_in = pl.ds(index * IN_HALF, 2 * IN_HALF)
@@ -233,14 +234,16 @@
                 factor = scale[rows_at((index - 1) * ny + start, BLOCK), :]
             lanes = slice(half * nz, (half + 1) * nz)
             for k, a in enumerate(corners):
+                at = rows_at((index - 1 + a) * ny + start, BLOCK)
                 for b in (0, 1):
                     for comp in range(3):
                         base = k * OUT_HALF + b * (OUT_HALF // 2) + comp * WINDOW
                         near = result[base : base + BLOCK, lanes] * factor
                         far = result[base + BLOCK : base + WINDOW, lanes] * factor
                         part = near + pltpu.roll(far, 1, 1)
-                        key = (index - 1 + a, b, comp, half)
-                        total[key] = total[key] + part if key in total else part
+                        if index - 1 + a in seen:
+                            part = part + force[b, comp, at, :]
+                        force[b, comp, at, :] = part
 
     count = jnp.full((1, nz), sub[0], jnp.int32)
     full_delta = coarse_step / count.astype(F32)
@@ -273,29 +276,40 @@
             w_gap[comp] = here
             w_fix[comp] = here * sign * inverse
 
-    def advance(step, carry):
-        slot = lax.rem(step, 2)
-        delta = jnp.where(step < count, full_delta, 0.0)
-        order = [lax.rem(step + i, n_pair) for i in range(n_pair)]
-
-        def arrive(q):
+    def advance(turn, carry):
+        for part in range(TURN):
+            one_step(turn, part)
+        return carry
+
+    def one_step(turn, part):
+        slot = part % 2
+        delta = jnp.where(turn * TURN + part < count, full_delta, 0.0)
+        order = [(part + i) % n_pair for i in range(n_pair)]
+        more = True if part < TURN - 1 else turn < MAXSUB // TURN - 1
+
+        def arrive(*pairs):
             @pl.when(d > 0)
             def _():
-                to_next(slot, q).wait_recv()
+                for q in pairs:
+                    to_next(slot, q).wait_recv()
 
             @pl.when(d < n_dom - 1)
             def _():
-                to_prev(slot, q).wait_recv()
+                for q in pairs:
+                    to_prev(slot, q).wait_recv()
+
+        def sent():
+            @pl.when(d > 0)
+            def _():
+                for q in order:
+                    to_prev(slot, q).wait_send()
+
+            @pl.when(d < n_dom - 1)
+            def _():
+                for q in order:
+                    to_next(slot, q).wait_send()
 
         def update(q):
-            @pl.when(d > 0)
-            def _():
-                to_prev(slot, q).wait_send()
-
-            @pl.when(d < n_dom - 1)
-            def _():
-                to_next(slot, q).wait_send()
-
             for plane in range(planes):
                 at = rows_at(plane * ny + q * WINDOW, WINDOW)
                 last = rows_at(plane * ny + before(q) * WINDOW + BLOCK, BLOCK)
@@ -307,11 +321,11 @@
                     o_v[comp, at, :] = speed
                     o_u[comp, at, :] = o_u[comp, at, :] + delta * speed
 
-            @pl.when((step < MAXSUB - 1) & (d > 0))
+            @pl.when((d > 0) & more)
             def _():
                 to_prev(1 - slot, q).start()
 
-            @pl.when((step < MAXSUB - 1) & (d < n_dom - 1))
+            @pl.when((d < n_dom - 1) & more)
             def _():
                 to_next(1 - slot, q).start()
 
@@ -323,26 +337,30 @@
             split_window(halo_rows(slot, 0), 0, q, odd)
             split_window(halo_rows(slot, 1), planes + 1, q, odd)
 
+        seen = set()
+        for index in range(1, planes):
+            for q in order:
+                layer(index, (0, 1), q, seen)
+            seen.update((index - 1, index))
         for i, q in enumerate(order):
-            total = {}
-            for index in range(1, planes):
-                layer(index, (0, 1), q, total)
             if i == 0:
-                @pl.when((step == 0) & (d > 0))
-                def _():
-                    scale_copy.wait_recv()
-
-                arrive(q)
+                if part == 0:
+                    @pl.when((turn == 0) & (d > 0))
+                    def _():
+                        scale_copy.wait_recv()
+
+                arrive(q, order[1])
+                sent()
                 halo_windows(q, False)
+            elif i < n_pair - 1:
+                arrive(order[i + 1])
             if i < n_pair - 1:
-                arrive(order[i + 1])
                 halo_windows(order[i + 1], False)
             halo_windows(q, True)
-            layer(0, (1,), q, total)
-            layer(planes, (0,), q, total)
-            for (plane, b, comp, half), part in total.items():
-                at = rows_at(plane * ny + q * WINDOW + half * BLOCK, BLOCK)
-                force[b, comp, at, :] = part
+            fresh = set(seen)
+            layer(0, (1,), q, fresh)
+            fresh.add(0)
+            layer(planes, (0,), q, fresh)
             if i > 0:
                 update(q)
                 own_windows(q, False)
@@ -353,13 +371,12 @@
         own_windows(order[0], True)
         own_windows(order[-1], True)
 
-        @pl.when(step == 0)
-        def _():
-            prepare()
-
-        return carry
-
-    lax.fori_loop(0, MAXSUB, advance, 0)
+        if part == 0:
+            @pl.when(turn == 0)
+            def _():
+                prepare()
+
+    lax.fori_loop(0, MAXSUB // TURN, advance, 0)
 
     for comp in range(3):
         for i in range(two):

time: 61.6 us -> 55.4 us (0.90)
  Pallas kernels: 57.7 us -> 51.4 us
    pallas_call x1, Pallas kernels: 57.7 us -> 51.4 us  [on_device(): pl.pallas_call(functools.partial(kernel, (n_grp, n_dom, planes, ny, nz, n...]
where the time goes in v3:
time: 55.4 us; the launch traced here: 55.2 us
  Pallas kernels  51.4 us (93%)
  local copies, waits for them, and re-layouts  2.46 us (4%)
  between operations  1.3 us (2%)
    pallas_call x1, Pallas kernels, on_device(): pl.pallas_call(functools.partial(kernel, (n_grp, n_dom, planes, ny, nz, n...  51.4 us
    unnamed x4, local copies, waits for them, and re-layouts  2.46 us

profile of v3, /device:TPU:0, one launch (start us, length us, event | category | flops | bytes accessed | tf_op | source)
XLA Modules:
  0.0 55.2 jit_solution(17398657188331183211)
XLA Ops:
  1.3 51.4 %shard_map.122 = (f32[3,192,128]{2,1,0:T(8,128)}, f32[3,192,128]{2,1,0:T(8,128)}) custom-call(f32[3,192,128]{2,1,0:T(8,128)} %bitcast.9, f32[3,192,128]{2,1,0:T(8,128)} %bitcast.10, f32[3,192,128]{2,1,0:T(8,128)} %bitcast.11, f32[192,128]{1,0:T(8,128)} %bitcast.14, f32[192,128]{1,0:T(8,128)} %bitcast.15, f32[24,24]{1,0:T(8,128)} %bitcast.16, ...), custom_call_target="tpu_custom_call" | custom-call | tf_op jit(solution)/shard_map/pallas_call | solution.py:470
  52.7 0.0 copy-start
  52.7 1.7 %copy.16 = f32[1,3,2,96,128]{4,3,2,1,0:T(8,128)} copy(f32[1,3,2,96,128]{4,3,2,1,0:T(8,128)} %bitcast.13) | data formatting | bytes 589824
  54.5 0.0 copy-done
  54.5 0.7 %copy.17 = f32[1,3,2,96,128]{4,3,2,1,0:T(8,128)} copy(f32[1,3,2,96,128]{4,3,2,1,0:T(8,128)S(1)} %bitcast.12) | data formatting | bytes 589824
Async XLA Ops:
  52.7 1.8 %copy-start = (f32[3,192,128]{2,1,0:T(8,128)S(1)}, f32[3,192,128]{2,1,0:T(8,128)}, u32[]{:S(2)}) copy-start(f32[3,192,128]{2,1,0:T(8,128)} %get-tuple-element.5) | copy-start | bytes 884740
